TPU v7x, 32 devices: a whole 2x2x4 slice. The times are simulated.
32 devices in a mesh: fsdp: 4 (over y, x), seq: 8 (over z, core).
Axes of the slice: x: 2, y: 2, z: 4, core: 2. Of those that a mesh axis runs over, the one named last changes fastest.
Arguments:
- tokens: bfloat16 [8, 1024, 2048], P('fsdp', 'seq'), may hold values from -6 to 6
- positions: int32 [8, 1024], P('fsdp', 'seq'), may hold values from 0 to 2046, as said below
- gain_attn: bfloat16 [2048], P('fsdp'), may hold values from 0.099609375 to 1.8984375
- w_query: bfloat16 [2048, 2048], P('fsdp'), may hold values from -0.1875 to 0.1875
- w_key: bfloat16 [2048, 512], P('fsdp'), may hold values from -0.1875 to 0.1875
- w_value: bfloat16 [2048, 512], P('fsdp'), may hold values from -0.125 to 0.125
- w_out: bfloat16 [2048, 2048], P('fsdp'), may hold values from -0.5 to 0.5
- gain_ffn: bfloat16 [2048], P('fsdp'), may hold values from 0.099609375 to 1.8984375
- w_gate: bfloat16 [2048, 8192], P('fsdp'), may hold values from -0.125 to 0.125
- w_up: bfloat16 [2048, 8192], P('fsdp'), may hold values from -0.125 to 0.125
- w_down: bfloat16 [8192, 2048], P('fsdp'), may hold values from -0.0625 to 0.0625
- grad_out: bfloat16 [8, 1024, 2048], P('fsdp', 'seq'), may hold values from -6 to 6
Outputs:
- layer_out: bfloat16 [8, 1024, 2048], P('fsdp', 'seq')
- grad_tokens: bfloat16 [8, 1024, 2048], P('fsdp', 'seq')
- grad_gain_attn: float32 [2048], P('fsdp')
- grad_w_query: float32 [2048, 2048], P('fsdp')
- grad_w_key: float32 [2048, 512], P('fsdp')
- grad_w_value: float32 [2048, 512], P('fsdp')
- grad_w_out: float32 [2048, 2048], P('fsdp')
- grad_gain_ffn: float32 [2048], P('fsdp')
- grad_w_gate: float32 [2048, 8192], P('fsdp')
- grad_w_up: float32 [2048, 8192], P('fsdp')
- grad_w_down: float32 [8192, 2048], P('fsdp')
Inputs may be any that keep to these rules, and one draw needn't show every extreme that they name: Along each sequence the positions rise strictly, by 1 or 2 from one token to the next.
All inputs are finite; a program needn't handle non-finite values.
Results may differ from a plain program's by a relative error of at most 0.02.
Values may be sent and summed in bfloat16 or wider, within the bound.
No kernel may reach another device: no remote copies, remote signals or barrier semaphores. Data moves between devices by JAX's collectives and lax.ppermute only.
A program may use at most 512 MiB of HBM per device.

v0:
```python
import math
import jax
import jax.numpy as jnp
from jax import lax
from jax.sharding import PartitionSpec as P

HEADS = 32
KV_HEADS = 8
HEAD_DIM = 64
norm_eps = 1e-05
theta_log = math.log(500000.0)


def rope_tables(places, half_dim):
    freqs = jnp.exp(jnp.arange(half_dim, dtype=jnp.float32) * (-2.0 * theta_log / (2 * half_dim)))
    angles = places.astype(jnp.float32)[..., None] * freqs
    return (jnp.cos(angles), jnp.sin(angles))


def rotate(field, cos_tab, sin_tab):
    half_dim = field.shape[-1] // 2
    lower_half = field[..., :half_dim]
    upper_half = field[..., half_dim:]
    return jnp.concatenate(
        [lower_half * cos_tab - upper_half * sin_tab, upper_half * cos_tab + lower_half * sin_tab],
        -1,
    )


def unrotate(field, cos_tab, sin_tab):
    half_dim = field.shape[-1] // 2
    lower_half = field[..., :half_dim]
    upper_half = field[..., half_dim:]
    return jnp.concatenate(
        [lower_half * cos_tab + upper_half * sin_tab, upper_half * cos_tab - lower_half * sin_tab],
        -1,
    )


def times_transposed(inputs, weight):
    return lax.dot_general(
        inputs, weight, (((1,), (1,)), ((), ())), preferred_element_type=jnp.float32
    )


def rows_of(inputs, grads):
    return lax.psum_scatter(
        lax.dot_general(
            inputs, grads, (((0,), (0,)), ((), ())), preferred_element_type=jnp.float32
        ).astype(jnp.bfloat16),
        "fsdp",
        scatter_dimension=0,
        tiled=True,
    ).astype(jnp.float32)


def body(
    tokens,
    positions,
    gain_attn,
    w_query,
    w_key,
    w_value,
    w_out,
    gain_ffn,
    w_gate,
    w_up,
    w_down,
    grad_out,
):
    seq_count, tok_span, width = tokens.shape
    tok_rows = seq_count * tok_span
    seq_devs = lax.axis_size("seq")
    copies = max(KV_HEADS, seq_devs)
    repeats = copies // KV_HEADS
    q_local = HEADS // seq_devs
    kv_local = copies // seq_devs
    per_copy = HEADS // copies
    full_len = tok_span * seq_devs
    block_len = min(512, full_len)
    n_blocks = full_len // block_len
    logit_scale = HEAD_DIM ** (-0.5)
    gain_a, wq_all, wk_all, wv_all, wo_all, gain_f = (
        lax.all_gather(gain_attn, "fsdp", axis=0, tiled=True),
        lax.all_gather(w_query, "fsdp", axis=0, tiled=True),
        lax.all_gather(w_key, "fsdp", axis=0, tiled=True),
        lax.all_gather(w_value, "fsdp", axis=0, tiled=True),
        lax.all_gather(w_out, "fsdp", axis=0, tiled=True),
        lax.all_gather(gain_ffn, "fsdp", axis=0, tiled=True),
    )
    x_float = tokens.reshape(tok_rows, width).astype(jnp.float32)
    inv_one = lax.rsqrt(jnp.mean(x_float * x_float, -1, keepdims=True) + norm_eps)
    x_hat = x_float * inv_one
    gain_one = gain_a.astype(jnp.float32)
    normed_one = (x_hat * gain_one).astype(jnp.bfloat16)
    query = jnp.dot(normed_one, wq_all, preferred_element_type=jnp.float32).reshape(
        tok_rows, HEADS, HEAD_DIM
    )
    key_raw = jnp.dot(normed_one, wk_all, preferred_element_type=jnp.float32).reshape(
        tok_rows, KV_HEADS, HEAD_DIM
    )
    value_raw = jnp.dot(normed_one, wv_all, preferred_element_type=jnp.float32).reshape(
        tok_rows, KV_HEADS, HEAD_DIM
    )
    cos_tab, sin_tab = rope_tables(positions.reshape(tok_rows), HEAD_DIM // 2)
    cos_tab = cos_tab[:, None, :]
    sin_tab = sin_tab[:, None, :]
    q_rot = (
        rotate(query, cos_tab, sin_tab)
        .astype(jnp.bfloat16)
        .reshape(seq_count, tok_span, HEADS * HEAD_DIM)
    )
    k_rot = rotate(key_raw, cos_tab, sin_tab).astype(jnp.bfloat16)
    v_low = value_raw.astype(jnp.bfloat16)
    kv_pair = jnp.stack([jnp.repeat(k_rot, repeats, 1), jnp.repeat(v_low, repeats, 1)], 2)
    kv_pair = kv_pair.reshape(seq_count, tok_span, copies * 2 * HEAD_DIM)
    q_heads, kv_heads = (
        lax.all_to_all(q_rot, "seq", split_axis=2, concat_axis=1, tiled=True),
        lax.all_to_all(kv_pair, "seq", split_axis=2, concat_axis=1, tiled=True),
    )
    q_heads = q_heads.reshape(seq_count, full_len, kv_local, per_copy, HEAD_DIM)
    kv_heads = kv_heads.reshape(seq_count, full_len, kv_local, 2, HEAD_DIM)
    k_heads = kv_heads[:, :, :, 0]
    v_heads = kv_heads[:, :, :, 1]
    key_index = jnp.arange(full_len, dtype=jnp.int32)

    def block_logits(offset):
        q_block = lax.dynamic_slice_in_dim(q_heads, offset, block_len, 1)
        logits = (
            jnp.einsum("sqcgd,skcd->scgqk", q_block, k_heads, preferred_element_type=jnp.float32)
            * logit_scale
        )
        query_index = offset + jnp.arange(block_len, dtype=jnp.int32)
        allowed = key_index[None, :] <= query_index[:, None]
        return (q_block, jnp.where(allowed, logits, -1e30))

    def forward_block(block_idx, state_pair):
        attended, log_sums = state_pair
        offset = block_idx * block_len
        _, logits = block_logits(offset)
        row_max = jnp.max(logits, -1, keepdims=True)
        weights_exp = jnp.exp(logits - row_max)
        row_sum = jnp.sum(weights_exp, -1, keepdims=True)
        prob_low = (weights_exp / row_sum).astype(jnp.bfloat16)
        block_out = jnp.einsum(
            "scgqk,skcd->sqcgd", prob_low, v_heads, preferred_element_type=jnp.float32
        )
        block_out = block_out.astype(jnp.bfloat16).reshape(seq_count, block_len, q_local * HEAD_DIM)
        attended = lax.dynamic_update_slice_in_dim(attended, block_out, offset, 1)
        log_sums = lax.dynamic_update_slice_in_dim(log_sums, row_max + jnp.log(row_sum), offset, 3)
        return (attended, log_sums)

    empty_out = jnp.zeros((seq_count, full_len, q_local * HEAD_DIM), jnp.bfloat16)
    empty_lse = jnp.zeros((seq_count, kv_local, per_copy, full_len, 1), jnp.float32)
    attended, log_sums = lax.fori_loop(0, n_blocks, forward_block, (empty_out, empty_lse))
    o_tokens = lax.all_to_all(attended, "seq", split_axis=1, concat_axis=2, tiled=True).reshape(
        tok_rows, HEADS * HEAD_DIM
    )
    resid = x_float + jnp.dot(o_tokens, wo_all, preferred_element_type=jnp.float32)
    inv_two = lax.rsqrt(jnp.mean(resid * resid, -1, keepdims=True) + norm_eps)
    resid_hat = resid * inv_two
    gain_two = gain_f.astype(jnp.float32)
    normed_two = (resid_hat * gain_two).astype(jnp.bfloat16)
    pieces = (
        lax.all_gather(w_gate, "fsdp", axis=0, tiled=True),
        lax.all_gather(w_up, "fsdp", axis=0, tiled=True),
    )
    columns = normed_two
    gate = jnp.dot(columns, pieces[0], preferred_element_type=jnp.float32)
    upper = jnp.dot(columns, pieces[1], preferred_element_type=jnp.float32)
    gate_sig = jax.nn.sigmoid(gate)
    gate_act = gate * gate_sig
    hidden = (gate_act * upper).astype(jnp.bfloat16)
    columns = hidden
    branch_out = jnp.dot(
        columns,
        lax.all_gather(w_down, "fsdp", axis=0, tiled=True),
        preferred_element_type=jnp.float32,
    )
    layer_out = (resid + branch_out).astype(jnp.bfloat16).reshape(seq_count, tok_span, width)
    cot_rows = grad_out.reshape(tok_rows, width)
    grad_down = rows_of(hidden, cot_rows)
    d_hidden = times_transposed(cot_rows, lax.all_gather(w_down, "fsdp", axis=0, tiled=True))
    d_gate = (d_hidden * upper * (gate_sig + gate_act * (1.0 - gate_sig))).astype(jnp.bfloat16)
    d_up = (d_hidden * gate_act).astype(jnp.bfloat16)
    grad_gate = rows_of(normed_two, d_gate)
    grad_upper = rows_of(normed_two, d_up)
    pieces = lax.all_gather((w_gate, w_up), "fsdp", axis=0, tiled=True)
    d_normed_two = times_transposed(d_gate, pieces[0]) + times_transposed(d_up, pieces[1])
    d_hat_two = d_normed_two * gain_two
    grad_gain_two = jnp.sum(d_normed_two * resid_hat, 0)
    d_resid = cot_rows.astype(jnp.float32) + inv_two * (
        d_hat_two - resid_hat * jnp.mean(d_hat_two * resid_hat, -1, keepdims=True)
    )
    d_branch = d_resid.astype(jnp.bfloat16)
    grad_out_w = lax.dot_general(
        o_tokens, d_branch, (((0,), (0,)), ((), ())), preferred_element_type=jnp.float32
    )
    d_attended = (
        times_transposed(d_branch, wo_all)
        .astype(jnp.bfloat16)
        .reshape(seq_count, tok_span, HEADS * HEAD_DIM)
    )
    d_heads = lax.all_to_all(d_attended, "seq", split_axis=2, concat_axis=1, tiled=True)
    d_heads = d_heads.reshape(seq_count, full_len, kv_local, per_copy, HEAD_DIM)

    def backward_block(block_idx, state_three):
        d_query_h, d_key_h, d_value_h = state_three
        offset = block_idx * block_len
        q_block, logits = block_logits(offset)
        probs = jnp.exp(logits - lax.dynamic_slice_in_dim(log_sums, offset, block_len, 3))
        prob_low = probs.astype(jnp.bfloat16)
        grad_block = lax.dynamic_slice_in_dim(d_heads, offset, block_len, 1)
        d_probs = jnp.einsum(
            "sqcgd,skcd->scgqk", grad_block, v_heads, preferred_element_type=jnp.float32
        )
        inner = jnp.sum(probs * d_probs, -1, keepdims=True)
        d_logits = (probs * (d_probs - inner)).astype(jnp.bfloat16)
        dq_block = (
            jnp.einsum("scgqk,skcd->sqcgd", d_logits, k_heads, preferred_element_type=jnp.float32)
            * logit_scale
        )
        d_key_h = (
            d_key_h
            + jnp.einsum("scgqk,sqcgd->skcd", d_logits, q_block, preferred_element_type=jnp.float32)
            * logit_scale
        )
        d_value_h = d_value_h + jnp.einsum(
            "scgqk,sqcgd->skcd", prob_low, grad_block, preferred_element_type=jnp.float32
        )
        d_query_h = lax.dynamic_update_slice_in_dim(
            d_query_h, dq_block.astype(jnp.bfloat16), offset, 1
        )
        return (d_query_h, d_key_h, d_value_h)

    empty_dq = jnp.zeros((seq_count, full_len, kv_local, per_copy, HEAD_DIM), jnp.bfloat16)
    empty_dkv = jnp.zeros((seq_count, full_len, kv_local, HEAD_DIM), jnp.float32)
    d_query_h, d_key_h, d_value_h = lax.fori_loop(
        0, n_blocks, backward_block, (empty_dq, empty_dkv, empty_dkv)
    )
    d_kv_pair = (
        jnp.stack([d_key_h, d_value_h], 3)
        .astype(jnp.bfloat16)
        .reshape(seq_count, full_len, kv_local * 2 * HEAD_DIM)
    )
    d_q_pack = d_query_h.reshape(seq_count, full_len, q_local * HEAD_DIM)
    dq_tokens, dkv_tokens = (
        lax.all_to_all(d_q_pack, "seq", split_axis=1, concat_axis=2, tiled=True),
        lax.all_to_all(d_kv_pair, "seq", split_axis=1, concat_axis=2, tiled=True),
    )
    dq_rot = dq_tokens.reshape(tok_rows, HEADS, HEAD_DIM).astype(jnp.float32)
    dkv_sum = jnp.sum(
        dkv_tokens.reshape(tok_rows, KV_HEADS, repeats, 2, HEAD_DIM).astype(jnp.float32), 2
    )
    d_query = (
        unrotate(dq_rot, cos_tab, sin_tab).astype(jnp.bfloat16).reshape(tok_rows, HEADS * HEAD_DIM)
    )
    d_key = (
        unrotate(dkv_sum[:, :, 0], cos_tab, sin_tab)
        .astype(jnp.bfloat16)
        .reshape(tok_rows, KV_HEADS * HEAD_DIM)
    )
    d_value = dkv_sum[:, :, 1].astype(jnp.bfloat16).reshape(tok_rows, KV_HEADS * HEAD_DIM)
    d_qkv = jnp.concatenate([d_query, d_key, d_value], 1)
    grad_qkv = lax.dot_general(
        normed_one, d_qkv, (((0,), (0,)), ((), ())), preferred_element_type=jnp.float32
    )
    q_width = HEADS * HEAD_DIM
    kv_width = KV_HEADS * HEAD_DIM
    grad_query = grad_qkv[:, :q_width]
    grad_key = grad_qkv[:, q_width : q_width + kv_width]
    grad_value = grad_qkv[:, q_width + kv_width :]
    d_normed_one = (
        times_transposed(d_query, wq_all)
        + times_transposed(d_key, wk_all)
        + times_transposed(d_value, wv_all)
    )
    d_hat_one = d_normed_one * gain_one
    grad_gain_one = jnp.sum(d_normed_one * x_hat, 0)
    d_input = d_resid + inv_one * (
        d_hat_one - x_hat * jnp.mean(d_hat_one * x_hat, -1, keepdims=True)
    )
    grad_tokens = d_input.astype(jnp.bfloat16).reshape(seq_count, tok_span, width)
    sum_q, sum_k, sum_v, sum_o, sum_g1, sum_g2 = (
        lax.psum_scatter(
            grad_query.astype(jnp.bfloat16), "fsdp", scatter_dimension=0, tiled=True
        ).astype(jnp.float32),
        lax.psum_scatter(
            grad_key.astype(jnp.bfloat16), "fsdp", scatter_dimension=0, tiled=True
        ).astype(jnp.float32),
        lax.psum_scatter(
            grad_value.astype(jnp.bfloat16), "fsdp", scatter_dimension=0, tiled=True
        ).astype(jnp.float32),
        lax.psum_scatter(
            grad_out_w.astype(jnp.bfloat16), "fsdp", scatter_dimension=0, tiled=True
        ).astype(jnp.float32),
        lax.psum_scatter(
            grad_gain_one.astype(jnp.bfloat16), "fsdp", scatter_dimension=0, tiled=True
        ).astype(jnp.float32),
        lax.psum_scatter(
            grad_gain_two.astype(jnp.bfloat16), "fsdp", scatter_dimension=0, tiled=True
        ).astype(jnp.float32),
    )
    all_q, all_k, all_v, all_o, all_g1, all_g2, all_gate, all_up, all_down = (
        lax.psum(sum_q.astype(jnp.bfloat16), "seq").astype(jnp.float32),
        lax.psum(sum_k.astype(jnp.bfloat16), "seq").astype(jnp.float32),
        lax.psum(sum_v.astype(jnp.bfloat16), "seq").astype(jnp.float32),
        lax.psum(sum_o.astype(jnp.bfloat16), "seq").astype(jnp.float32),
        lax.psum(sum_g1.astype(jnp.bfloat16), "seq").astype(jnp.float32),
        lax.psum(sum_g2.astype(jnp.bfloat16), "seq").astype(jnp.float32),
        lax.psum(grad_gate.astype(jnp.bfloat16), "seq").astype(jnp.float32),
        lax.psum(grad_upper.astype(jnp.bfloat16), "seq").astype(jnp.float32),
        lax.psum(grad_down.astype(jnp.bfloat16), "seq").astype(jnp.float32),
    )
    return (
        layer_out,
        grad_tokens,
        all_g1,
        all_q,
        all_k,
        all_v,
        all_o,
        all_g2,
        all_gate,
        all_up,
        all_down,
    )


def solution(mesh):
    placed = (
        P("fsdp", "seq", None),
        P("fsdp", "seq"),
        P("fsdp"),
        P("fsdp", None),
        P("fsdp", None),
        P("fsdp", None),
        P("fsdp", None),
        P("fsdp"),
        P("fsdp", None),
        P("fsdp", None),
        P("fsdp", None),
        P("fsdp", "seq", None),
    )
    return jax.shard_map(
        body,
        mesh=mesh,
        in_specs=placed,
        out_specs=(
            P("fsdp", "seq", None),
            P("fsdp", "seq", None),
            P("fsdp"),
            P("fsdp", None),
            P("fsdp", None),
            P("fsdp", None),
            P("fsdp", None),
            P("fsdp"),
            P("fsdp", None),
            P("fsdp", None),
            P("fsdp", None),
        ),
        check_vma=False,
    )
```

profile of v0, /device:TPU:0, one launch (start us, length us, event | category | flops | bytes accessed | tf_op | source)
XLA Modules:
  0.0 3219.5 jit_solution(10981159727728233364)
XLA Ops:
  11.9 9.5 all-gather
  22.9 25.0 all-gather.14.cloned.1.call-done
  50.9 34.2 %all-gather.12.cloned.1.call-done = bf16[2048,512]{1,0:T(8,128)(2,1)} async-done(((bf16[512,512]{1,0:T(8,128)(2,1)}), bf16[2048,512]{1,0:T(8,128)(2,1)}) %all-gather.12.cloned.1.call-update) | async-done | bytes 2097168 | tf_op jit(solution)/shard_map/all_gather | solution.py:86
  97.8 76.8 %all-gather.10.cloned.1.call-done = bf16[2048,2048]{1,0:T(8,128)(2,1)} async-done(((bf16[512,2048]{1,0:T(8,128)(2,1)}), bf16[2048,2048]{1,0:T(8,128)(2,1)}) %all-gather.10.cloned.1.call-update) | async-done | bytes 8388624 | tf_op jit(solution)/shard_map/all_gather | solution.py:85
  174.6 12.3 copy.52
  200.2 25.9 all-to-all-done
  229.3 30.2 while.34
  264.2 8.1 all-gather.1
  272.3 18.4 all-to-all-done.2
  299.4 263.4 %all-gather.18.cloned.1.call-done = bf16[2048,8192]{1,0:T(8,128)(2,1)} async-done(((bf16[512,8192]{1,0:T(8,128)(2,1)}), bf16[2048,8192]{1,0:T(8,128)(2,1)}) %all-gather.18.cloned.1.call-update) | async-done | bytes 33554448 | tf_op jit(solution)/shard_map/all_gather | solution.py:165
  562.9 21.9 fusion.80
  584.8 277.0 %all-gather.20.cloned.1.call-done = bf16[2048,8192]{1,0:T(8,128)(2,1)} async-done(((bf16[512,8192]{1,0:T(8,128)(2,1)}), bf16[2048,8192]{1,0:T(8,128)(2,1)}) %all-gather.20.cloned.1.call-update) | async-done | bytes 33554448 | tf_op jit(solution)/shard_map/all_gather | solution.py:166
  861.8 21.2 fusion.81
  883.1 277.8 %all-gather.22.cloned.1.call-done = bf16[8192,2048]{1,0:T(8,128)(2,1)} async-done(((bf16[2048,2048]{1,0:T(8,128)(2,1)}), bf16[8192,2048]{1,0:T(8,128)(2,1)}) %all-gather.22.cloned.1.call-update) | async-done | bytes 33554448 | tf_op jit(solution)/shard_map/all_gather | solution.py:177
  1160.9 23.0 multiply_convert_fusion
  1183.9 17.5 fusion.82
  1201.3 18.7 multiply_reduce_fusion
  1222.4 6.5 convolution_convert_fusion.5
  1235.6 26.6 all-to-all-done.3
  1265.2 98.1 %while.35 = (s32[]{:T(128)}, bf16[2,1024,1,4,64]{1,4,3,0,2:T(8,128)(2,1)}, f32[2,1024,1,64]{1,3,0,2:T(8,128)}, f32[2,1024,1,64]{1,3,0,2:T(8,128)}, bf16[2,1024,1...) while((s32[]{:T(128)}, ...), condition=%wide.region_9.10_spmd.clone, body=%wide.region_7.0_spmd.clone.sunk | while | flops 2748969472 | bytes 213307824 | solution.py:238
  1271.1 11.3 fusion.154
  1282.4 10.7 fusion.155
  1293.1 6.9 fusion.156
  1305.3 8.2 fusion.158
  1320.1 11.3 fusion.154
  1331.4 10.7 fusion.155
  1342.1 6.9 fusion.156
  1354.3 8.2 fusion.158
  1373.3 11.6 all-to-all-done.5
  1391.8 23.2 all-to-all-done.4
  1431.6 7.8 convolution_convert_fusion.3
  1445.5 7.0 convolution_convert_fusion.4
  1452.5 8.7 slice.77
  1461.3 16.6 convolution_convert_fusion.2
  1478.0 16.9 convolution_convert_fusion.1
  1495.1 16.4 convolution_convert_fusion
  1515.6 89.9 %reduce-scatter.20.cloned.1.call-done = bf16[512,2048]{1,0:T(8,128)(2,1)} async-done(((bf16[2048,2048]{1,0:T(8,128)(2,1)}), bf16[512,2048]{1,0:T(8,128)(2,1)}) %reduce-scatter.20.cloned.1.call-update) | async-done | bytes 2097168 | tf_op jit(solution)/shard_map/reduce_scatter | solution.py:294
  1605.5 90.4 %reduce-scatter.14.cloned.1.call-done = bf16[512,2048]{1,0:T(8,128)(2,1)} async-done(((bf16[2048,2048]{1,0:T(8,128)(2,1)}), bf16[512,2048]{1,0:T(8,128)(2,1)}) %reduce-scatter.14.cloned.1.call-update) | async-done | bytes 2097168 | tf_op jit(solution)/shard_map/reduce_scatter | solution.py:285
  1695.9 291.6 %reduce-scatter.22.cloned.1.call-done = bf16[512,8192]{1,0:T(8,128)(2,1)} async-done(((bf16[2048,8192]{1,0:T(8,128)(2,1)}), bf16[512,8192]{1,0:T(8,128)(2,1)}) %reduce-scatter.22.cloned.1.call-update) | async-done | bytes 8388624
  1987.5 292.0 %reduce-scatter.24.cloned.1.call-done = bf16[512,8192]{1,0:T(8,128)(2,1)} async-done(((bf16[2048,8192]{1,0:T(8,128)(2,1)}), bf16[512,8192]{1,0:T(8,128)(2,1)}) %reduce-scatter.24.cloned.1.call-update) | async-done | bytes 8388624
  2279.6 291.6 %reduce-scatter.26.cloned.1.call-done = bf16[2048,2048]{1,0:T(8,128)(2,1)} async-done(((bf16[8192,2048]{1,0:T(8,128)(2,1)}), bf16[2048,2048]{1,0:T(8,128)(2,1)}) %reduce-scatter.26.cloned.1.call-update) | async-done | bytes 8388624
  2573.0 19.2 fusion.62
  2592.2 9.1 all-reduce.7
  2601.4 15.8 all-reduce.5
  2621.5 547.0 %all-reduce.10.cloned.1.call-done = (bf16[512,2048]{1,0:T(8,128)(2,1)}, bf16[512,512]{1,0:T(8,128)(2,1)}, bf16[512,512]{1,0:T(8,128)(2,1)}, bf16[512,2048]{1,0:T...) async-done(((bf16[512,2048]{1,0:T(8,128)(2,1)}, bf16[512,512]{1,0:T(8,128)(2,1)}, bf16[512,512]{1,0:T(8,128)(2,1)}, ...) | async-done | bytes 30408720 | tf_op jit(solution)/shard_map/psum | solution.py:305
  3177.6 11.7 convert_element_type.289
  3189.3 11.7 convert_element_type.291
  3201.0 11.7 convert_element_type.293
  (224 shorter events, 175.7 us)
Async XLA Ops:
  7.2 40.7 %all-gather.14.cloned.1.call-start = ((), (), s32[]{:S(2)}) async-start(), calls=%async_computation.15 | async-start | bytes 2621440 | tf_op jit(solution)/shard_map/all_gather | solution.py:87
  7.9 77.2 %all-gather.12.cloned.1.call-start = ((), (), s32[]{:S(2)}) async-start(), calls=%async_computation.14 | async-start | bytes 2621440 | tf_op jit(solution)/shard_map/all_gather | solution.py:86
  8.7 165.9 %all-gather.10.cloned.1.call-start = ((), (), s32[]{:S(2)}) async-start(), calls=%async_computation.13 | async-start | bytes 10485760 | tf_op jit(solution)/shard_map/all_gather | solution.py:85
  9.4 282.2 %all-gather.16.cloned.1.call-start = ((), (), s32[]{:S(2)}) async-start(), calls=%async_computation.16 | async-start | bytes 10485760 | tf_op jit(solution)/shard_map/all_gather | solution.py:88
  10.0 552.9 %all-gather.18.cloned.1.call-start = ((), (), s32[]{:S(2)}) async-start(), calls=%async_computation.17 | async-start | bytes 41943040 | tf_op jit(solution)/shard_map/all_gather | solution.py:165
  10.6 851.3 %all-gather.20.cloned.1.call-start = ((), (), s32[]{:S(2)}) async-start(), calls=%async_computation.18 | async-start | bytes 41943040 | tf_op jit(solution)/shard_map/all_gather | solution.py:166
  11.1 10.4 copy-start.5
  11.2 11.2 copy-start.34
  11.2 1149.7 %all-gather.22.cloned.1.call-start = ((), (), s32[]{:S(2)}) async-start(), calls=%async_computation.19 | async-start | bytes 41943040 | tf_op jit(solution)/shard_map/all_gather | solution.py:177
  21.5 26.4 copy-start.28
  22.6 170.5 %copy-start.20 = (f32[256,32]{0,1:T(8,128)}, f32[256,32]{0,1:T(8,128)S(1)}, u32[]{:S(2)}) copy-start(f32[256,32]{0,1:T(8,128)S(1)} %get-tuple-element.425) | copy-start | bytes 98308
  22.6 170.5 %copy-start.22 = (f32[256,32]{0,1:T(8,128)}, f32[256,32]{0,1:T(8,128)S(1)}, u32[]{:S(2)}) copy-start(f32[256,32]{0,1:T(8,128)S(1)} %get-tuple-element.426) | copy-start | bytes 98308
  93.2 101.4 %all-to-all-start.1 = ((bf16[2,128,1024]{1,0,2:T(2,128)(2,1)}), bf16[2,128,1024]{1,0,2:T(2,128)(2,1)S(1)}, u32[]{:S(2)}, u32[]{:S(2)}) async-start(bf16[2,128,1024]{1,0,2:T(2,128)(2,1)} %reshape.420), calls=%async_computation.1 | async-start | bytes 1048576 | tf_op jit(solution)/shard_map/all_to_all | solution.py:119
  194.6 31.5 all-to-all-start
  229.3 34.9 %copy-start.33 = (bf16[512]{0:T(512)(128)(2,1)S(1)}, bf16[512]{0:T(512)(128)(2,1)}, u32[]{:S(2)}) copy-start(bf16[512]{0:T(512)(128)(2,1)} %param.23) | copy-start | bytes 3076
  260.5 31.2 copy-start.6
  260.5 30.2 all-to-all-start.2
  291.6 6.3 copy-start.14
  299.4 562.4 %copy-start.9 = (bf16[256,2048]{1,0:T(8,128)(2,1)}, bf16[256,2048]{1,0:T(8,128)(2,1)S(1)}, u32[]{:S(2)}) copy-start(bf16[256,2048]{1,0:T(8,128)(2,1)S(1)} %multiply_convert_fusion.4) | copy-start | bytes 3145732
  584.8 576.1 %copy-start.15 = (bf16[2,128,2048]{2,1,0:T(8,128)(2,1)S(1)}, bf16[2,128,2048]{2,1,0:T(8,128)(2,1)}, u32[]{:S(2)}) copy-start(bf16[2,128,2048]{2,1,0:T(8,128)(2,1)} %param.27) | copy-start | bytes 3145732
  1183.9 17.5 copy-start.13
  1222.4 6.5 copy-start.3
  1231.0 31.2 all-to-all-start.3
  1268.8 13.6 copy-start
  1293.1 6.9 copy-start.1
  1300.0 5.3 copy-start.26
  1305.3 8.3 copy-start.2
  1317.8 13.6 copy-start
  1342.1 6.9 copy-start.1
  1349.0 5.3 copy-start.26
  1354.3 8.3 copy-start.2
  1366.0 25.0 copy-start.21
  1366.0 25.0 copy-start.23
  1366.0 18.9 all-to-all-start.5
  1384.9 30.1 all-to-all-start.4
  1388.5 123.1 %reduce-scatter.16.cloned.1.call-start = ((), (), s32[]{:S(2)}) async-start(), calls=%async_computation.21 | async-start | bytes 2621440 | tf_op jit(solution)/shard_map/reduce_scatter | solution.py:288
  1421.0 6.0 copy-start.11
  1421.0 6.0 copy-start.18
  1443.9 71.7 %reduce-scatter.18.cloned.1.call-start = ((), (), s32[]{:S(2)}) async-start(), calls=%async_computation.22 | async-start | bytes 2621440 | tf_op jit(solution)/shard_map/reduce_scatter | solution.py:291
  1444.6 160.9 %reduce-scatter.20.cloned.1.call-start = ((), (), s32[]{:S(2)}) async-start(), calls=%async_computation.23 | async-start | bytes 10485760 | tf_op jit(solution)/shard_map/reduce_scatter | solution.py:294
  1452.5 243.4 %reduce-scatter.14.cloned.1.call-start = ((), (), s32[]{:S(2)}) async-start(), calls=%async_computation.20 | async-start | bytes 10485760 | tf_op jit(solution)/shard_map/reduce_scatter | solution.py:285
  1461.3 526.2 %reduce-scatter.22.cloned.1.call-start = ((), (), s32[]{:S(2)}) async-start(), calls=%async_computation.24 | async-start | bytes 41943040
  1477.9 801.6 %reduce-scatter.24.cloned.1.call-start = ((), (), s32[]{:S(2)}) async-start(), calls=%async_computation.25 | async-start | bytes 41943040
  1494.9 1076.2 %reduce-scatter.26.cloned.1.call-start = ((), (), s32[]{:S(2)}) async-start(), calls=%async_computation.26 | async-start | bytes 41943040
  1511.5 1657.0 %all-reduce.10.cloned.1.call-start = ((), (), s32[]{:S(2)}) async-start(), calls=%async_computation.27 | async-start | bytes 60817408 | tf_op jit(solution)/shard_map/psum | solution.py:305
  2573.0 19.2 copy-start.31
  3168.5 5.4 copy-start.24
  3168.5 6.5 copy-start.19
  (16 other events, 39.4 us)
Sparse Core Ops, SparseCore 0:
  9.9 38.0 all-gather.13
  49.8 35.2 all-gather.11
  87.0 87.5 all-gather.9
  176.3 87.5 all-gather.15
  265.6 297.2 all-gather.17
  564.6 297.2 all-gather.19
  863.6 297.2 all-gather.21
  1444.0 33.0 reduce-scatter.15
  1480.4 35.1 reduce-scatter.17
  1519.1 86.3 reduce-scatter.19
  1609.5 86.4 reduce-scatter.13
  1698.8 288.6 reduce-scatter.21
  1990.9 288.6 reduce-scatter.23
  2282.5 288.6 reduce-scatter.25
  2574.8 593.6 all-reduce.9
where the time goes:
time: 3230 us; the launch traced here: 3220 us
  waiting for transfers between devices  2670 us (83%)
  matrix products  305 us (9%)
  other arithmetic  88.7 us (3%)
  local copies, waits for them, and re-layouts  69.2 us (2%)
  blocking collectives  42.4 us (1%)
    unnamed x18, waiting for transfers between devices  880 us
    psum x1, waiting for transfers between devices, body(): lax.psum(sum_q.astype(jnp.bfloat16), 'seq').astype(jnp.float32)  547 us
    all_gather x1, waiting for transfers between devices, body(): lax.all_gather(w_down, 'fsdp', axis=0, tiled=True)  278 us
    all_gather x1, waiting for transfers between devices, body(): lax.all_gather(w_up, 'fsdp', axis=0, tiled=True)  277 us
    all_gather x1, waiting for transfers between devices, body(): lax.all_gather(w_gate, 'fsdp', axis=0, tiled=True)  263 us
    reduce_scatter x1, waiting for transfers between devices, body(): lax.psum_scatter(grad_query.astype(jnp.bfloat16), 'fsdp', scatter_dimensi...  90.4 us
    reduce_scatter x1, waiting for transfers between devices, body(): lax.psum_scatter(grad_out_w.astype(jnp.bfloat16), 'fsdp', scatter_dimensi...  89.9 us
    all_gather x1, waiting for transfers between devices, body(): lax.all_gather(w_query, 'fsdp', axis=0, tiled=True)  76.8 us
  transfers between devices with their start and end apart: 21, of which 18 were waited for; matrix products, arithmetic and copies ran while one was open for 7% of the time, Pallas kernels for 0%

commit v1 on v0

--- a/solution.py
+++ b/solution.py
@@ -301,8 +301,12 @@
             grad_gain_two.astype(jnp.bfloat16), "fsdp", scatter_dimension=0, tiled=True
         ).astype(jnp.float32),
     )
+
+    def proceed_the_tasks(point, axis_name):
+        return jnp.sum(lax.all_gather(point, axis_name=axis_name), 0)
+
     all_q, all_k, all_v, all_o, all_g1, all_g2, all_gate, all_up, all_down = (
-        lax.psum(sum_q.astype(jnp.bfloat16), "seq").astype(jnp.float32),
+        proceed_the_tasks(sum_q.astype(jnp.bfloat16), "seq").astype(jnp.float32),
         lax.psum(sum_k.astype(jnp.bfloat16), "seq").astype(jnp.float32),
         lax.psum(sum_v.astype(jnp.bfloat16), "seq").astype(jnp.float32),
         lax.psum(sum_o.astype(jnp.bfloat16), "seq").astype(jnp.float32),

time: 3230 us -> 3340 us (1.034)
  waiting for transfers between devices: 2670 us -> 2770 us
    all_gather x0 -> x1, waiting for transfers between devices: none -> 101 us  [proceed_the_tasks(): return jnp.sum(lax.all_gather(point, axis_name=axis_name), 0)]
    reduce_scatter x1, waiting for transfers between devices: 90.4 us -> 19.7 us  [body(): lax.psum_scatter(grad_query.astype(jnp.bfloat16), 'fsdp', scatter_dimensi...]
    reduce_scatter x1, waiting for transfers between devices: 0.02 us -> 38.4 us  [body(): lax.psum_scatter(grad_key.astype(jnp.bfloat16), 'fsdp', scatter_dimension...]
    reduce_scatter x1, waiting for transfers between devices: 4.03 us -> 38 us  [body(): lax.psum_scatter(grad_value.astype(jnp.bfloat16), 'fsdp', scatter_dimensi...]
    unnamed x18 -> x19, waiting for transfers between devices: 880 us -> 880 us
  transfers between devices with their start and end apart: 21 -> 22, of which waited for: 18 -> 20; matrix products, arithmetic and copies ran while one was open for 7% -> 7% of each run, Pallas kernels for 0% -> 0%
where the time goes in v1:
time: 3340 us; the launch traced here: 3330 us
  waiting for transfers between devices  2770 us (83%)
  matrix products  308 us (9%)
  other arithmetic  99.6 us (3%)
  local copies, waits for them, and re-layouts  69.2 us (2%)
  blocking collectives  42.4 us (1%)
    unnamed x19, waiting for transfers between devices  880 us
    psum x1, waiting for transfers between devices, body(): lax.psum(sum_k.astype(jnp.bfloat16), 'seq').astype(jnp.float32)  542 us
    all_gather x1, waiting for transfers between devices, body(): lax.all_gather(w_down, 'fsdp', axis=0, tiled=True)  278 us
    all_gather x1, waiting for transfers between devices, body(): lax.all_gather(w_up, 'fsdp', axis=0, tiled=True)  277 us
    all_gather x1, waiting for transfers between devices, body(): lax.all_gather(w_gate, 'fsdp', axis=0, tiled=True)  263 us
    all_gather x1, waiting for transfers between devices, proceed_the_tasks(): return jnp.sum(lax.all_gather(point, axis_name=axis_name), 0)  101 us
    reduce_scatter x1, waiting for transfers between devices, body(): lax.psum_scatter(grad_out_w.astype(jnp.bfloat16), 'fsdp', scatter_dimensi...  90.4 us
    all_gather x1, waiting for transfers between devices, body(): lax.all_gather(w_query, 'fsdp', axis=0, tiled=True)  76.8 us
  transfers between devices with their start and end apart: 22, of which 20 were waited for; matrix products, arithmetic and copies ran while one was open for 7% of the time, Pallas kernels for 0%

profile of v1, /device:TPU:0, one launch (start us, length us, event | category | flops | bytes accessed | tf_op | source)
XLA Modules:
  0.0 3331.4 jit_solution(6209017977008992249)
XLA Ops:
  11.9 9.5 all-gather.1
  22.9 25.0 all-gather.16.cloned.1.call-done
  50.9 34.2 %all-gather.14.cloned.1.call-done = bf16[2048,512]{1,0:T(8,128)(2,1)} async-done(((bf16[512,512]{1,0:T(8,128)(2,1)}), bf16[2048,512]{1,0:T(8,128)(2,1)}) %all-gather.14.cloned.1.call-update) | async-done | bytes 2097168 | tf_op jit(solution)/shard_map/all_gather | solution.py:86
  97.8 76.8 %all-gather.12.cloned.1.call-done = bf16[2048,2048]{1,0:T(8,128)(2,1)} async-done(((bf16[512,2048]{1,0:T(8,128)(2,1)}), bf16[2048,2048]{1,0:T(8,128)(2,1)}) %all-gather.12.cloned.1.call-update) | async-done | bytes 8388624 | tf_op jit(solution)/shard_map/all_gather | solution.py:85
  174.6 12.3 copy.52
  200.2 25.9 all-to-all-done
  229.3 30.3 while.34
  264.2 8.1 all-gather.2
  272.3 18.4 all-to-all-done.2
  299.5 263.4 %all-gather.20.cloned.1.call-done = bf16[2048,8192]{1,0:T(8,128)(2,1)} async-done(((bf16[512,8192]{1,0:T(8,128)(2,1)}), bf16[2048,8192]{1,0:T(8,128)(2,1)}) %all-gather.20.cloned.1.call-update) | async-done | bytes 33554448 | tf_op jit(solution)/shard_map/all_gather | solution.py:165
  562.9 21.9 fusion.80
  584.8 277.0 %all-gather.22.cloned.1.call-done = bf16[2048,8192]{1,0:T(8,128)(2,1)} async-done(((bf16[512,8192]{1,0:T(8,128)(2,1)}), bf16[2048,8192]{1,0:T(8,128)(2,1)}) %all-gather.22.cloned.1.call-update) | async-done | bytes 33554448 | tf_op jit(solution)/shard_map/all_gather | solution.py:166
  861.8 21.2 fusion.81
  883.1 277.8 %all-gather.24.cloned.1.call-done = bf16[8192,2048]{1,0:T(8,128)(2,1)} async-done(((bf16[2048,2048]{1,0:T(8,128)(2,1)}), bf16[8192,2048]{1,0:T(8,128)(2,1)}) %all-gather.24.cloned.1.call-update) | async-done | bytes 33554448 | tf_op jit(solution)/shard_map/all_gather | solution.py:177
  1160.9 22.9 multiply_convert_fusion
  1183.8 17.5 fusion.82
  1201.3 18.7 multiply_reduce_fusion
  1235.6 26.6 all-to-all-done.3
  1265.2 98.2 %while.35 = (s32[]{:T(128)}, bf16[2,1024,1,4,64]{1,4,3,0,2:T(8,128)(2,1)}, f32[2,1024,1,64]{1,3,0,2:T(8,128)}, f32[2,1024,1,64]{1,3,0,2:T(8,128)}, bf16[2,1024,1...) while((s32[]{:T(128)}, ...), condition=%wide.region_9.10_spmd.clone, body=%wide.region_7.0_spmd.clone.sunk | while | flops 2748969472 | bytes 213307824 | solution.py:238
  1271.1 11.3 fusion.154
  1282.4 10.7 fusion.155
  1305.4 8.2 fusion.158
  1320.1 11.3 fusion.154
  1331.4 10.7 fusion.155
  1354.4 8.2 fusion.158
  1373.3 11.6 all-to-all-done.5
  1391.9 23.2 all-to-all-done.4
  1431.7 7.8 convolution_convert_fusion.3
  1439.5 8.4 slice.77
  1461.3 17.5 convolution_convert_fusion.2
  1478.8 16.9 convolution_convert_fusion.1
  1496.0 16.7 convolution_convert_fusion
  1512.7 19.7 reduce-scatter.14.cloned.1.call-done
  1532.5 38.4 %reduce-scatter.16.cloned.1.call-done = bf16[512,512]{1,0:T(8,128)(2,1)} async-done(((bf16[2048,512]{1,0:T(8,128)(2,1)}), bf16[512,512]{1,0:T(8,128)(2,1)}) %reduce-scatter.16.cloned.1.call-update) | async-done | bytes 524304 | tf_op jit(solution)/shard_map/reduce_scatter | solution.py:288
  1570.9 38.0 %reduce-scatter.18.cloned.1.call-done = bf16[512,512]{1,0:T(8,128)(2,1)} async-done(((bf16[2048,512]{1,0:T(8,128)(2,1)}), bf16[512,512]{1,0:T(8,128)(2,1)}) %reduce-scatter.18.cloned.1.call-update) | async-done | bytes 524304 | tf_op jit(solution)/shard_map/reduce_scatter | solution.py:291
  1608.9 90.4 %reduce-scatter.20.cloned.1.call-done = bf16[512,2048]{1,0:T(8,128)(2,1)} async-done(((bf16[2048,2048]{1,0:T(8,128)(2,1)}), bf16[512,2048]{1,0:T(8,128)(2,1)}) %reduce-scatter.20.cloned.1.call-update) | async-done | bytes 2097168 | tf_op jit(solution)/shard_map/reduce_scatter | solution.py:294
  1699.3 291.6 %reduce-scatter.22.cloned.1.call-done = bf16[512,8192]{1,0:T(8,128)(2,1)} async-done(((bf16[2048,8192]{1,0:T(8,128)(2,1)}), bf16[512,8192]{1,0:T(8,128)(2,1)}) %reduce-scatter.22.cloned.1.call-update) | async-done | bytes 8388624
  1990.9 292.0 %reduce-scatter.24.cloned.1.call-done = bf16[512,8192]{1,0:T(8,128)(2,1)} async-done(((bf16[2048,8192]{1,0:T(8,128)(2,1)}), bf16[512,8192]{1,0:T(8,128)(2,1)}) %reduce-scatter.24.cloned.1.call-update) | async-done | bytes 8388624
  2282.9 291.6 %reduce-scatter.26.cloned.1.call-done = bf16[2048,2048]{1,0:T(8,128)(2,1)} async-done(((bf16[8192,2048]{1,0:T(8,128)(2,1)}), bf16[2048,2048]{1,0:T(8,128)(2,1)}) %reduce-scatter.26.cloned.1.call-update) | async-done | bytes 8388624
  2576.4 20.5 fusion.62
  2596.9 9.0 all-reduce.7
  2606.0 15.8 all-reduce.5
  2626.2 101.3 %all-gather.26.cloned.1.call-done = bf16[4096,2048]{1,0:T(8,128)(2,1)} async-done(((bf16[512,2048]{1,0:T(8,128)(2,1)}), bf16[4096,2048]{1,0:T(8,128)(2,1)}) %all-gather.26.cloned.1.call-update) | async-done | bytes 16777232 | tf_op jit(solution)/shard_map/all_gather | solution.py:306
  2727.5 10.4 reduce_sum.97
  2740.4 542.1 %all-reduce.10.cloned.1.call-done = (bf16[512,512]{1,0:T(8,128)(2,1)}, bf16[512,512]{1,0:T(8,128)(2,1)}, bf16[512,2048]{1,0:T(8,128)(2,1)}, bf16[512,8192]{1,0:T...) async-done(((bf16[512,512]{1,0:T(8,128)(2,1)}, bf16[512,512]{1,0:T(8,128)(2,1)}, bf16[512,2048]{1,0:T(8,128)(2,1)}, bf16[512,8192]{1,0:T(8,128)(2,1)}, ...) | async-done | bytes 28311568 | tf_op jit(solution)/shard_map/psum | solution.py:310
  3289.4 11.7 convert_element_type.291
  3301.2 11.7 convert_element_type.293
  3312.9 11.7 convert_element_type.295
  (224 shorter events, 199.8 us)
Async XLA Ops:
  7.2 40.7 %all-gather.16.cloned.1.call-start = ((), (), s32[]{:S(2)}) async-start(), calls=%async_computation.15 | async-start | bytes 2621440 | tf_op jit(solution)/shard_map/all_gather | solution.py:87
  7.9 77.2 %all-gather.14.cloned.1.call-start = ((), (), s32[]{:S(2)}) async-start(), calls=%async_computation.14 | async-start | bytes 2621440 | tf_op jit(solution)/shard_map/all_gather | solution.py:86
  8.7 165.9 %all-gather.12.cloned.1.call-start = ((), (), s32[]{:S(2)}) async-start(), calls=%async_computation.13 | async-start | bytes 10485760 | tf_op jit(solution)/shard_map/all_gather | solution.py:85
  9.4 282.3 %all-gather.18.cloned.1.call-start = ((), (), s32[]{:S(2)}) async-start(), calls=%async_computation.16 | async-start | bytes 10485760 | tf_op jit(solution)/shard_map/all_gather | solution.py:88
  10.0 552.9 %all-gather.20.cloned.1.call-start = ((), (), s32[]{:S(2)}) async-start(), calls=%async_computation.17 | async-start | bytes 41943040 | tf_op jit(solution)/shard_map/all_gather | solution.py:165
  10.6 851.3 %all-gather.22.cloned.1.call-start = ((), (), s32[]{:S(2)}) async-start(), calls=%async_computation.18 | async-start | bytes 41943040 | tf_op jit(solution)/shard_map/all_gather | solution.py:166
  11.1 10.4 copy-start.5
  11.2 11.2 copy-start.32
  11.2 1149.7 %all-gather.24.cloned.1.call-start = ((), (), s32[]{:S(2)}) async-start(), calls=%async_computation.19 | async-start | bytes 41943040 | tf_op jit(solution)/shard_map/all_gather | solution.py:177
  21.5 26.4 copy-start.26
  22.6 170.5 %copy-start.20 = (f32[256,32]{0,1:T(8,128)}, f32[256,32]{0,1:T(8,128)S(1)}, u32[]{:S(2)}) copy-start(f32[256,32]{0,1:T(8,128)S(1)} %get-tuple-element.424) | copy-start | bytes 98308
  22.6 170.5 %copy-start.22 = (f32[256,32]{0,1:T(8,128)}, f32[256,32]{0,1:T(8,128)S(1)}, u32[]{:S(2)}) copy-start(f32[256,32]{0,1:T(8,128)S(1)} %get-tuple-element.425) | copy-start | bytes 98308
  93.2 101.4 %all-to-all-start.1 = ((bf16[2,128,1024]{1,0,2:T(2,128)(2,1)}), bf16[2,128,1024]{1,0,2:T(2,128)(2,1)S(1)}, u32[]{:S(2)}, u32[]{:S(2)}) async-start(bf16[2,128,1024]{1,0,2:T(2,128)(2,1)} %reshape.420), calls=%async_computation.1 | async-start | bytes 1048576 | tf_op jit(solution)/shard_map/all_to_all | solution.py:119
  194.6 31.5 all-to-all-start
  229.3 34.9 %copy-start.31 = (bf16[512]{0:T(512)(128)(2,1)S(1)}, bf16[512]{0:T(512)(128)(2,1)}, u32[]{:S(2)}) copy-start(bf16[512]{0:T(512)(128)(2,1)} %param.23) | copy-start | bytes 3076
  260.5 31.2 copy-start.6
  260.5 30.2 all-to-all-start.2
  291.6 6.3 copy-start.14
  299.5 562.4 %copy-start.9 = (bf16[256,2048]{1,0:T(8,128)(2,1)}, bf16[256,2048]{1,0:T(8,128)(2,1)S(1)}, u32[]{:S(2)}) copy-start(bf16[256,2048]{1,0:T(8,128)(2,1)S(1)} %multiply_convert_fusion.4) | copy-start | bytes 3145732
  584.8 576.1 %copy-start.15 = (bf16[2,128,2048]{2,1,0:T(8,128)(2,1)S(1)}, bf16[2,128,2048]{2,1,0:T(8,128)(2,1)}, u32[]{:S(2)}) copy-start(bf16[2,128,2048]{2,1,0:T(8,128)(2,1)} %param.27) | copy-start | bytes 3145732
  1183.8 17.5 copy-start.13
  1222.4 6.5 copy-start.3
  1230.9 31.2 all-to-all-start.3
  1268.8 13.6 copy-start
  1293.1 6.9 copy-start.1
  1300.0 5.3 copy-start.24
  1305.3 8.3 copy-start.2
  1317.8 13.6 copy-start
  1342.1 6.9 copy-start.1
  1349.0 5.3 copy-start.17
  1349.0 5.3 copy-start.24
  1354.3 8.3 copy-start.2
  1366.1 25.0 copy-start.21
  1366.1 25.0 copy-start.23
  1366.1 18.9 all-to-all-start.5
  1385.0 30.1 all-to-all-start.4
  1388.5 143.9 %reduce-scatter.14.cloned.1.call-start = ((), (), s32[]{:S(2)}) async-start(), calls=%async_computation.20 | async-start | bytes 10485760 | tf_op jit(solution)/shard_map/reduce_scatter | solution.py:285
  1421.1 6.0 copy-start.11
  1421.1 6.0 copy-start.18
  1447.9 123.0 %reduce-scatter.16.cloned.1.call-start = ((), (), s32[]{:S(2)}) async-start(), calls=%async_computation.21 | async-start | bytes 2621440 | tf_op jit(solution)/shard_map/reduce_scatter | solution.py:288
  1452.5 156.4 %reduce-scatter.18.cloned.1.call-start = ((), (), s32[]{:S(2)}) async-start(), calls=%async_computation.22 | async-start | bytes 2621440 | tf_op jit(solution)/shard_map/reduce_scatter | solution.py:291
  1453.1 246.2 %reduce-scatter.20.cloned.1.call-start = ((), (), s32[]{:S(2)}) async-start(), calls=%async_computation.23 | async-start | bytes 10485760 | tf_op jit(solution)/shard_map/reduce_scatter | solution.py:294
  1461.2 529.7 %reduce-scatter.22.cloned.1.call-start = ((), (), s32[]{:S(2)}) async-start(), calls=%async_computation.25 | async-start | bytes 41943040
  1478.7 804.2 %reduce-scatter.24.cloned.1.call-start = ((), (), s32[]{:S(2)}) async-start(), calls=%async_computation.26 | async-start | bytes 41943040
  1495.7 1078.8 %reduce-scatter.26.cloned.1.call-start = ((), (), s32[]{:S(2)}) async-start(), calls=%async_computation.27 | async-start | bytes 41943040
  1512.7 1214.8 %all-gather.26.cloned.1.call-start = ((), (), s32[]{:S(2)}) async-start(), calls=%async_computation.24 | async-start | bytes 18874368 | tf_op jit(solution)/shard_map/all_gather | solution.py:306
  1532.4 1750.0 %all-reduce.10.cloned.1.call-start = ((), (), s32[]{:S(2)}) async-start(), calls=%async_computation.28 | async-start | bytes 56623104 | tf_op jit(solution)/shard_map/psum | solution.py:310
  2576.4 20.5 copy-start.29
  (15 other events, 34.4 us)
Sparse Core Ops, SparseCore 0:
  9.9 38.0 all-gather.15
  49.8 35.2 all-gather.13
  87.0 87.5 all-gather.11
  176.3 87.5 all-gather.17
  265.6 297.2 all-gather.19
  564.6 297.2 all-gather.21
  863.6 297.2 all-gather.23
  1448.0 84.3 reduce-scatter.13
  1535.6 35.1 reduce-scatter.15
  1573.7 35.1 reduce-scatter.17
  1612.9 86.4 reduce-scatter.19
  1702.2 288.6 reduce-scatter.21
  1994.2 288.6 reduce-scatter.23
  2285.9 288.6 reduce-scatter.25
  2576.0 151.3 all-gather.25
  2730.9 551.4 all-reduce.9
